TPU v7x, 32 devices: a whole 2x2x4 slice. The times are simulated.
32 devices in a mesh: dp: 16 (over z, y, core), mp: 2 (over x).
Axes of the slice: x: 2, y: 2, z: 4, core: 2. Of those that a mesh axis runs over, the one named last changes fastest.
Arguments:
- tokens: bfloat16 [16384, 1024], P('dp', 'mp'), may hold values from -6 to 6
- cotangent: bfloat16 [16384, 1024], P('dp', 'mp'), may hold values from -6 to 6
- route: int32 [16384], P('dp'), may hold values from 0 to 16383, as said below
- seq_lengths: int32 [16, 4], P('dp'), may hold values from 1 to 512, 1024 in all within a row
- norm1_gain: float32 [1024], replicated, may hold values from 0.25 to 1.75
- in_weight: bfloat16 [3, 1024, 1024], P(None, None, 'mp'), may hold values from -0.1875 to 0.1875
- conv_weight: float32 [3, 1024], P(None, 'mp'), may hold values from -3 to 3
- out_weight: bfloat16 [1024, 1024], P('mp'), may hold values from -0.1875 to 0.1875
- norm2_gain: float32 [1024], replicated, may hold values from 0.25 to 1.75
- gate_weight: bfloat16 [1024, 4608], P(None, 'mp'), may hold values from -0.1875 to 0.1875
- up_weight: bfloat16 [1024, 4608], P(None, 'mp'), may hold values from -0.1875 to 0.1875
- down_weight: bfloat16 [4608, 1024], P('mp'), may hold values from -0.09375 to 0.09375
Outputs:
- block_out: bfloat16 [16384, 1024], P('dp', 'mp')
- tokens_grad: float32 [16384, 1024], P('dp', 'mp')
- norm1_gain_grad: float32 [1024], replicated
- in_weight_grad: float32 [3, 1024, 1024], P(None, None, 'mp')
- conv_weight_grad: float32 [3, 1024], P(None, 'mp')
- out_weight_grad: float32 [1024, 1024], P('mp')
- norm2_gain_grad: float32 [1024], replicated
- gate_weight_grad: float32 [1024, 4608], P(None, 'mp')
- up_weight_grad: float32 [1024, 4608], P(None, 'mp')
- down_weight_grad: float32 [4608, 1024], P('mp')
Inputs may be any that keep to these rules, and one draw needn't show every extreme that they name: route is a permutation of the packed places; the 1024 arrival rows of one dp shard go 96 to one group, 32 to another and 64 to each other group, which groups drawn from the seed. `seq_lengths`: each row sums to 1024.
All inputs are finite; a program needn't handle non-finite values.
Results may differ from a plain program's by a relative error of at most 0.011.
Values may be sent and summed in bfloat16 or wider, within the bound.
No kernel may reach another device: no remote copies, remote signals or barrier semaphores. Data moves between devices by JAX's collectives and lax.ppermute only.
A program may use at most 192 MiB of HBM per device.

v0:
```python
import jax
import jax.numpy as jnp
from jax import lax
from jax.sharding import PartitionSpec as P

epsilon = 1e-05


def lag_rows(values, shift):
    return jnp.concatenate(
        [jnp.zeros((shift, values.shape[1]), values.dtype), values[:-shift]], axis=0
    )


def lead_rows(values, shift):
    return jnp.concatenate(
        [values[shift:], jnp.zeros((shift, values.shape[1]), values.dtype)], axis=0
    )


def seq_masks(lengths, row_count):
    starts = jnp.cumsum(lengths, dtype=jnp.int32) - lengths
    position = jnp.arange(row_count, dtype=jnp.int32)
    started = position[:, None] >= starts[None, :]
    seq_first = jnp.max(jnp.where(started, starts[None, :], 0), axis=1)
    offset = position - seq_first
    return ((offset >= 1).astype(jnp.float32)[:, None], (offset >= 2).astype(jnp.float32)[:, None])


def padded_piece(piece, start, model_width):
    return lax.dynamic_update_slice_in_dim(jnp.zeros((model_width,), jnp.float32), piece, start, 0)


def on_device(
    tokens,
    cotangent,
    route,
    seq_lengths,
    norm1_gain,
    in_weight,
    conv_weight,
    out_weight,
    norm2_gain,
    gate_weight,
    up_weight,
    down_weight,
):
    dp_size = lax.axis_size("dp")
    mp_index = lax.axis_index("mp")
    row_count = tokens.shape[0]
    narrow = tokens.shape[1]
    model_width = norm1_gain.shape[0]
    pair_share = row_count // dp_size
    slot_count = pair_share + pair_share // 2
    ordering = jnp.argsort(route)
    target = route[ordering] // row_count
    members = jnp.arange(dp_size, dtype=jnp.int32)
    counts = jnp.sum(
        (target[:, None] == members[None, :]).astype(jnp.int32), axis=0, dtype=jnp.int32
    )
    begins = jnp.cumsum(counts, dtype=jnp.int32) - counts
    slot_ids = jnp.arange(slot_count, dtype=jnp.int32)
    filled = slot_ids[None, :] < counts[:, None]
    sources = ordering[jnp.clip(begins[:, None] + slot_ids[None, :], 0, row_count - 1)]
    pulled_rows = tokens[sources]
    pulled_seeds = cotangent[sources]
    send_rows = jnp.where(filled[:, :, None], pulled_rows, jnp.zeros_like(pulled_rows))
    send_seeds = jnp.where(filled[:, :, None], pulled_seeds, jnp.zeros_like(pulled_seeds))
    send_places = jnp.where(filled, route[sources] % row_count, row_count)
    got_rows, got_seeds, got_places = (
        lax.all_to_all(send_rows, "dp", split_axis=0, concat_axis=0, tiled=True),
        lax.all_to_all(send_seeds, "dp", split_axis=0, concat_axis=0, tiled=True),
        lax.all_to_all(send_places, "dp", split_axis=0, concat_axis=0, tiled=True),
    )
    flat_places = got_places.reshape(-1)
    input_piece = (
        jnp.zeros((row_count, narrow), tokens.dtype)
        .at[flat_places]
        .set(got_rows.reshape(-1, narrow), mode="drop")
    )
    seed_piece = (
        jnp.zeros((row_count, narrow), cotangent.dtype)
        .at[flat_places]
        .set(got_seeds.reshape(-1, narrow), mode="drop")
    )
    input_full, seed_full = (
        lax.all_gather(input_piece, "mp", axis=1, tiled=True),
        lax.all_gather(seed_piece, "mp", axis=1, tiled=True),
    )
    first_mask, second_mask = seq_masks(seq_lengths[0], row_count)
    column_start = mp_index * narrow
    gain_one = lax.dynamic_slice_in_dim(norm1_gain, column_start, narrow)
    gain_two = lax.dynamic_slice_in_dim(norm2_gain, column_start, narrow)
    residual = input_full.astype(jnp.float32)
    residual_piece = input_piece.astype(jnp.float32)
    scale_one = lax.rsqrt(jnp.mean(residual * residual, axis=1) + epsilon)
    normed_one = (residual * scale_one[:, None] * norm1_gain).astype(jnp.bfloat16)
    projected = jnp.einsum("rd,kdc->krc", normed_one, in_weight, preferred_element_type=jnp.float32)
    in_gate, out_gate, value_part = (projected[0], projected[1], projected[2])
    mixed = in_gate * value_part
    lag_one = lag_rows(mixed, 1) * first_mask
    lag_two = lag_rows(mixed, 2) * second_mask
    convolved = conv_weight[2] * mixed + conv_weight[1] * lag_one + conv_weight[0] * lag_two
    gated = (out_gate * convolved).astype(jnp.bfloat16)
    mix_terms = jnp.dot(gated, out_weight, preferred_element_type=jnp.float32)
    middle = residual_piece + lax.psum_scatter(mix_terms, "mp", scatter_dimension=1, tiled=True)
    square_sum = lax.psum(jnp.sum(middle * middle, axis=1), "mp")
    scale_two = lax.rsqrt(square_sum / model_width + epsilon)
    normed_piece = (middle * scale_two[:, None] * gain_two).astype(jnp.bfloat16)
    normed_two = lax.all_gather(normed_piece, "mp", axis=1, tiled=True)
    gate_val = jnp.dot(normed_two, gate_weight, preferred_element_type=jnp.float32)
    up_val = jnp.dot(normed_two, up_weight, preferred_element_type=jnp.float32)
    sigmoid_val = jax.nn.sigmoid(gate_val)
    silu_val = gate_val * sigmoid_val
    hidden = (silu_val * up_val).astype(jnp.bfloat16)
    down_terms = jnp.dot(hidden, down_weight, preferred_element_type=jnp.float32)
    block_piece = middle + lax.psum_scatter(down_terms, "mp", scatter_dimension=1, tiled=True)
    seed_local = seed_piece.astype(jnp.float32)
    grad_down = jnp.einsum("rf,rd->fd", hidden, seed_full, preferred_element_type=jnp.float32)
    grad_hidden = jnp.einsum(
        "rd,fd->rf", seed_full, down_weight, preferred_element_type=jnp.float32
    )
    grad_gate_val = (
        grad_hidden * up_val * sigmoid_val * (1.0 + gate_val * (1.0 - sigmoid_val))
    ).astype(jnp.bfloat16)
    grad_up_val = (grad_hidden * silu_val).astype(jnp.bfloat16)
    grad_gate = jnp.einsum(
        "rd,rf->df", normed_two, grad_gate_val, preferred_element_type=jnp.float32
    )
    grad_up = jnp.einsum("rd,rf->df", normed_two, grad_up_val, preferred_element_type=jnp.float32)
    normed_terms = jnp.einsum(
        "rf,df->rd", grad_gate_val, gate_weight, preferred_element_type=jnp.float32
    ) + jnp.einsum("rf,df->rd", grad_up_val, up_weight, preferred_element_type=jnp.float32)
    grad_normed_two = lax.psum_scatter(normed_terms, "mp", scatter_dimension=1, tiled=True)
    gain_two_piece = jnp.sum(grad_normed_two * middle * scale_two[:, None], axis=0)
    dot_two, grad_gain_two = lax.psum(
        (
            jnp.sum(gain_two * grad_normed_two * middle, axis=1),
            padded_piece(gain_two_piece, column_start, model_width),
        ),
        "mp",
    )
    grad_middle = (
        seed_local
        + scale_two[:, None] * gain_two * grad_normed_two
        - middle * (scale_two * scale_two * scale_two * dot_two / model_width)[:, None]
    )
    grad_mix_piece = grad_middle.astype(jnp.bfloat16)
    grad_mix = lax.all_gather(grad_mix_piece, "mp", axis=1, tiled=True)
    grad_out_weight = jnp.einsum("rc,rd->cd", gated, grad_mix, preferred_element_type=jnp.float32)
    grad_gated = jnp.einsum("rd,cd->rc", grad_mix, out_weight, preferred_element_type=jnp.float32)
    grad_conv = grad_gated * out_gate
    grad_conv_weight = jnp.stack(
        [
            jnp.sum(grad_conv * lag_two, axis=0),
            jnp.sum(grad_conv * lag_one, axis=0),
            jnp.sum(grad_conv * mixed, axis=0),
        ],
        axis=0,
    )
    grad_mixed = (
        conv_weight[2] * grad_conv
        + conv_weight[1] * lead_rows(grad_conv * first_mask, 1)
        + conv_weight[0] * lead_rows(grad_conv * second_mask, 2)
    )
    grad_parts = jnp.stack(
        [grad_mixed * value_part, grad_gated * convolved, grad_mixed * in_gate], axis=0
    ).astype(jnp.bfloat16)
    grad_in_weight = jnp.einsum(
        "rd,krc->kdc", normed_one, grad_parts, preferred_element_type=jnp.float32
    )
    first_terms = jnp.einsum(
        "krc,kdc->rd", grad_parts, in_weight, preferred_element_type=jnp.float32
    )
    grad_normed_one = lax.psum_scatter(first_terms, "mp", scatter_dimension=1, tiled=True)
    gain_one_piece = jnp.sum(grad_normed_one * residual_piece * scale_one[:, None], axis=0)
    dot_one, grad_gain_one = lax.psum(
        (
            jnp.sum(gain_one * grad_normed_one * residual_piece, axis=1),
            padded_piece(gain_one_piece, column_start, model_width),
        ),
        "mp",
    )
    input_grad = (
        grad_middle
        + scale_one[:, None] * gain_one * grad_normed_one
        - residual_piece * (scale_one * scale_one * scale_one * dot_one / model_width)[:, None]
    )
    summed = lax.psum(
        (
            grad_gain_one,
            grad_in_weight,
            grad_conv_weight,
            grad_out_weight,
            grad_gain_two,
            grad_gate,
            grad_up,
            grad_down,
        ),
        "dp",
    )
    local_ids = jnp.clip(got_places, 0, row_count - 1)
    back_out, back_grad = (
        lax.all_to_all(block_piece[local_ids], "dp", split_axis=0, concat_axis=0, tiled=True),
        lax.all_to_all(input_grad[local_ids], "dp", split_axis=0, concat_axis=0, tiled=True),
    )
    home = jnp.where(filled, sources, row_count).reshape(-1)
    block_out = (
        jnp.zeros((row_count, narrow), jnp.float32)
        .at[home]
        .set(back_out.reshape(-1, narrow), mode="drop")
        .astype(jnp.bfloat16)
    )
    tokens_grad = (
        jnp.zeros((row_count, narrow), jnp.float32)
        .at[home]
        .set(back_grad.reshape(-1, narrow), mode="drop")
    )
    return (
        block_out,
        tokens_grad,
        summed[0],
        summed[1],
        summed[2],
        summed[3],
        summed[4],
        summed[5],
        summed[6],
        summed[7],
    )


def solution(mesh):
    in_specs = (
        P("dp", "mp"),
        P("dp", "mp"),
        P("dp"),
        P("dp", None),
        P(),
        P(None, None, "mp"),
        P(None, "mp"),
        P("mp", None),
        P(),
        P(None, "mp"),
        P(None, "mp"),
        P("mp", None),
    )
    out_specs = (
        P("dp", "mp"),
        P("dp", "mp"),
        P(),
        P(None, None, "mp"),
        P(None, "mp"),
        P("mp", None),
        P(),
        P(None, "mp"),
        P(None, "mp"),
        P("mp", None),
    )
    return jax.shard_map(
        on_device, mesh=mesh, in_specs=in_specs, out_specs=out_specs, check_vma=False
    )
```

profile of v0, /device:TPU:0, one launch (start us, length us, event | category | flops | bytes accessed | tf_op | source)
XLA Modules:
  0.0 1352.7 jit_solution(5558362743720589754)
XLA Ops:
  63.2 30.1 %all-to-all-done.1 = bf16[16,96,512]{2,1,0:T(8,128)(2,1)} async-done(((bf16[16,96,512]{2,1,0:T(8,128)(2,1)}), bf16[16,96,512]{2,1,0:T(8,128)(2,1)}, u32[]{:S(2)}, u32[]{:S(2)}) %all-to-all-start.1) | async-done | bytes 1572896 | tf_op jit(solution)/shard_map/all_to_all | solution.py:71
  93.3 8.7 scatter_custom_fusion
  102.6 37.1 %all-gather.5.cloned.1.call-done = bf16[1024,1024]{1,0:T(8,128)(2,1)} async-done(((bf16[1024,512]{1,0:T(8,128)(2,1)}), bf16[1024,1024]{1,0:T(8,128)(2,1)}) %all-gather.5.cloned.1.call-update) | async-done | bytes 2097168 | tf_op jit(solution)/shard_map/all_gather | solution.py:87
  160.9 48.6 %reduce-scatter.5.cloned.1.call-done = f32[1024,512]{1,0:T(8,128)} async-done(((f32[1024,1024]{1,0:T(8,128)}), f32[1024,512]{1,0:T(8,128)}) %reduce-scatter.5.cloned.1.call-update) | async-done | bytes 2097168 | tf_op jit(solution)/shard_map/reduce_scatter | solution.py:106
  220.8 8.7 scatter_custom_fusion.2
  229.8 24.2 %all-gather.7.cloned.1.call-done = bf16[1024,1024]{1,0:T(8,128)(2,1)} async-done(((bf16[1024,512]{1,0:T(8,128)(2,1)}), bf16[1024,1024]{1,0:T(8,128)(2,1)}) %all-gather.7.cloned.1.call-update) | async-done | bytes 2097168 | tf_op jit(solution)/shard_map/all_gather | solution.py:110
  254.0 10.2 fusion.41
  264.2 9.9 fusion.40
  274.1 14.5 %all-gather.9.cloned.1.call-done = bf16[1024,1024]{1,0:T(8,128)(2,1)} async-done(((bf16[1024,512]{1,0:T(8,128)(2,1)}), bf16[1024,1024]{1,0:T(8,128)(2,1)}) %all-gather.9.cloned.1.call-update) | async-done | bytes 2097168 | tf_op jit(solution)/shard_map/all_gather | solution.py:88
  288.6 17.8 %multiply_convert_fusion = (bf16[1024,2304]{1,0:T(8,128)(2,1)}, bf16[1024,2304]{1,0:T(8,128)(2,1)}, bf16[1024,2304]{1,0:T(8,128)(2,1)}) fusion(f32[1024,2304]{1,0:T(8,128)} %fusion.40, f32[1024,2304]{1,0:T(8,128)} %fusion.41, bf16[1024,1024]{1,0:T(8,128)(2,1)} %all-gather.9.cloned.1.call-done, bf16[2304,1024]{1,0:T(8,128)(2,1)} %param.23), kind=kOutput, calls=%fused_computation.11 | convolution fusion | flops 4867227648 | bytes 39845888 | tf_op jit(solution)/shard_map/rd,fd->rf/dot_general | solution.py:120
  306.4 8.5 fusion.43
  314.9 9.0 convolution_add_fusion
  324.0 54.4 %reduce-scatter.9.cloned.1.call-done = f32[1024,512]{1,0:T(8,128)} async-done(((f32[1024,1024]{1,0:T(8,128)}), f32[1024,512]{1,0:T(8,128)}) %reduce-scatter.9.cloned.1.call-update) | async-done | bytes 2097168 | tf_op jit(solution)/shard_map/reduce_scatter | solution.py:134
  390.8 33.1 %all-gather.11.cloned.1.call-done = bf16[1024,1024]{1,0:T(8,128)(2,1)} async-done(((bf16[1024,512]{1,0:T(8,128)(2,1)}), bf16[1024,1024]{1,0:T(8,128)(2,1)}) %all-gather.11.cloned.1.call-update) | async-done | bytes 2097168 | tf_op jit(solution)/shard_map/all_gather | solution.py:149
  442.6 9.7 fusion.42
  452.6 10.3 fusion.47
  462.9 10.2 fusion.46
  473.1 10.3 fusion.45
  506.9 46.9 %reduce-scatter.7.cloned.1.call-done = f32[1024,512]{1,0:T(8,128)} async-done(((f32[1024,1024]{1,0:T(8,128)}), f32[1024,512]{1,0:T(8,128)}) %reduce-scatter.7.cloned.1.call-update) | async-done | bytes 2097168 | tf_op jit(solution)/shard_map/reduce_scatter | solution.py:117
  577.0 91.2 %all-to-all-done.2 = f32[16,96,512]{2,1,0:T(8,128)} async-done(((f32[16,96,512]{2,1,0:T(8,128)}), f32[16,96,512]{2,1,0:T(8,128)}, u32[]{:S(2)}, u32[]{:S(2)}) %all-to-all-start.2) | async-done | bytes 3145760 | tf_op jit(solution)/shard_map/all_to_all | solution.py:204
  668.2 12.8 all-to-all-start.4
  681.3 143.8 %all-reduce.4 = (f32[1024]{0:T(1024)}, f32[3,512]{1,0:T(4,128)}, f32[1024]{0:T(1024)}) all-reduce(f32[1024]{0:T(1024)S(1)} %get-tuple-element.68, f32[3,512]{1,0:T(4,128)S(1)} %pad_maximum_fusion.3, f32[1024]{0:T(1024)S(1)} %get-tuple-element.69), channel_id=1, replica_groups=mesh['dp'=16,'mp'=2] {'dp'}, use_global_device_ids=true, to_apply=%region_22.23 | all-reduce | flops 3584 | bytes 28672 | tf_op jit(solution)/shard_map/psum | solution.py:189
  834.3 9.0 scatter_custom_fusion.3
  843.3 473.7 %all-reduce.9.cloned.1.call-done = (f32[3,1024,512]{1,2,0:T(8,128)}, f32[512,1024]{1,0:T(8,128)}, f32[1024,2304]{1,0:T(8,128)}, f32[1024,2304]{1,0:T(8,128)}, f32[2304,1024]{1,0:T(8,128)}) async-done(((f32[3,1024,512]{1,2,0:T(8,128)}, f32[512,1024]{1,0:T(8,128)}, f32[1024,2304]{1,0:T(8,128)}, f32[1024,2304]{1,0:T(8,128)}, f32[2304,1024]{1,0:T(8,128)}), (f32[3,1024,512]{1,2,0:T(8,128)}, ...) | async-done | bytes 36700176 | tf_op jit(solution)/shard_map/psum | solution.py:189
  (186 shorter events, 205.1 us)
Async XLA Ops:
  7.2 134.9 %copy-start = (bf16[3,1024,512]{2,1,0:T(8,128)(2,1)S(1)}, bf16[3,1024,512]{2,1,0:T(8,128)(2,1)}, u32[]{:S(2)}) copy-start(bf16[3,1024,512]{2,1,0:T(8,128)(2,1)} %param.17) | copy-start | bytes 9437188
  17.1 21.0 %copy-start.24 = (s32[16]{0:T(128)}, s32[16]{0:T(128)S(1)}, u32[]{:S(2)}) copy-start(s32[16]{0:T(128)S(1)} %convert_reduce_fusion) | copy-start | bytes 196
  30.7 24.4 %all-to-all-start = ((s32[16,1,96]{2,1,0:T(1,128)}), s32[16,1,96]{2,1,0:T(1,128)S(1)}, u32[]{:S(2)}, u32[]{:S(2)}) async-start(s32[16,1,96]{2,1,0:T(1,128)} %compare_select_fusion.4), calls=%async_computation | async-start | bytes 16384 | tf_op jit(solution)/shard_map/all_to_all | solution.py:73
  55.1 47.2 %copy-start.32 = (s32[1,4]{1,0:T(1,128)S(1)}, s32[1,4]{1,0:T(1,128)}, u32[]{:S(2)}) copy-start(s32[1,4]{1,0:T(1,128)} %param.15) | copy-start | bytes 52
  55.1 47.5 %copy-start.26 = (f32[3,512]{1,0:T(4,128)S(1)}, f32[3,512]{1,0:T(4,128)}, u32[]{:S(2)}) copy-start(f32[3,512]{1,0:T(4,128)} %param.18) | copy-start | bytes 18436
  55.1 38.2 %all-to-all-start.1 = ((bf16[16,96,512]{2,1,0:T(8,128)(2,1)}), bf16[16,96,512]{2,1,0:T(8,128)(2,1)}, u32[]{:S(2)}, u32[]{:S(2)}) async-start(bf16[16,96,512]{2,1,0:T(8,128)(2,1)} %get-tuple-element.91), calls=%async_computation.1 | async-start | bytes 3145728 | tf_op jit(solution)/shard_map/all_to_all | solution.py:71
  61.3 78.5 %all-gather.5.cloned.1.call-start = ((), (), s32[]{:S(2)}) async-start(), calls=%async_computation.9 | async-start | bytes 3145728 | tf_op jit(solution)/shard_map/all_gather | solution.py:87
  93.3 48.7 %copy-start.28 = (f32[1024]{0:T(1024)S(1)}, f32[1024]{0:T(1024)}, u32[]{:S(2)}) copy-start(f32[1024]{0:T(1024)} %param.16) | copy-start | bytes 12292
  102.1 107.4 %reduce-scatter.5.cloned.1.call-start = ((), (), s32[]{:S(2)}) async-start(), calls=%async_computation.10 | async-start | bytes 6291456 | tf_op jit(solution)/shard_map/reduce_scatter | solution.py:106
  155.0 65.7 %all-to-all-start.3 = ((bf16[16,96,512]{2,1,0:T(8,128)(2,1)}), bf16[16,96,512]{2,1,0:T(8,128)(2,1)}, u32[]{:S(2)}, u32[]{:S(2)}) async-start(bf16[16,96,512]{2,1,0:T(8,128)(2,1)} %get-tuple-element.90), calls=%async_computation.5 | async-start | bytes 3145728 | tf_op jit(solution)/shard_map/all_to_all | solution.py:72
  160.7 93.3 %all-gather.7.cloned.1.call-start = ((), (), s32[]{:S(2)}) async-start(), calls=%async_computation.11 | async-start | bytes 3145728 | tf_op jit(solution)/shard_map/all_gather | solution.py:110
  220.7 67.9 %all-gather.9.cloned.1.call-start = ((), (), s32[]{:S(2)}) async-start(), calls=%async_computation.13 | async-start | bytes 3145728 | tf_op jit(solution)/shard_map/all_gather | solution.py:88
  229.5 148.9 %reduce-scatter.9.cloned.1.call-start = ((), (), s32[]{:S(2)}) async-start(), calls=%async_computation.14 | async-start | bytes 6291456 | tf_op jit(solution)/shard_map/reduce_scatter | solution.py:134
  323.9 99.9 %all-gather.11.cloned.1.call-start = ((), (), s32[]{:S(2)}) async-start(), calls=%async_computation.15 | async-start | bytes 3145728 | tf_op jit(solution)/shard_map/all_gather | solution.py:149
  390.6 106.5 %reduce-scatter.11.cloned.1.call-start = ((), (), s32[]{:S(2)}) async-start(), calls=%async_computation.16 | async-start | bytes 6291456 | tf_op jit(solution)/shard_map/reduce_scatter | solution.py:175
  442.6 111.2 %reduce-scatter.7.cloned.1.call-start = ((), (), s32[]{:S(2)}) async-start(), calls=%async_computation.12 | async-start | bytes 6291456 | tf_op jit(solution)/shard_map/reduce_scatter | solution.py:117
  452.4 864.7 %all-reduce.9.cloned.1.call-start = ((), (), s32[]{:S(2)}) async-start(), calls=%async_computation.17 | async-start | bytes 73400320 | tf_op jit(solution)/shard_map/psum | solution.py:189
  492.2 14.6 %copy-start.22 = (f32[1024]{0:T(1024)S(1)}, f32[1024]{0:T(1024)}, u32[]{:S(2)}) copy-start(f32[1024]{0:T(1024)} %copy-done.21) | copy-start | bytes 12292
  566.4 101.8 %all-to-all-start.2 = ((f32[16,96,512]{2,1,0:T(8,128)}), f32[16,96,512]{2,1,0:T(8,128)}, u32[]{:S(2)}, u32[]{:S(2)}) async-start(f32[16,96,512]{2,1,0:T(8,128)} %bitcast.104), calls=%async_computation.4 | async-start | bytes 6291456 | tf_op jit(solution)/shard_map/all_to_all | solution.py:204
  668.2 12.8 copy-start.20
  668.2 12.9 copy-start.25
  668.2 166.1 %all-to-all-start.4 = ((f32[16,96,512]{2,1,0:T(8,128)}), f32[16,96,512]{2,1,0:T(8,128)}, u32[]{:S(2)}, u32[]{:S(2)}) async-start(f32[16,96,512]{2,1,0:T(8,128)} %bitcast.103), calls=%async_computation.8 | async-start | bytes 6291456 | tf_op jit(solution)/shard_map/all_to_all | solution.py:205
  1325.1 16.5 %slice-start = ((s8[9437184]{0:T(1024)(128)(4,1)}), s8[4194304]{0:T(1024)(128)(4,1)S(1)}, s32[]{:S(2)}) async-start(s8[9437184]{0:T(1024)(128)(4,1)} %bitcast.105), calls=%async_computation.18 | async-start | bytes 8388608
  1325.1 16.5 %slice-start.1 = ((s8[9437184]{0:T(1024)(128)(4,1)}), s8[4194304]{0:T(1024)(128)(4,1)S(1)}, s32[]{:S(2)}) async-start(s8[9437184]{0:T(1024)(128)(4,1)} %bitcast.105), calls=%async_computation.19 | async-start | bytes 8388608
  (27 other events, 134.0 us)
Sparse Core Ops, SparseCore 0:
  102.2 37.5 all-gather.4
  155.1 54.2 reduce-scatter.4
  220.8 33.1 all-gather.6
  255.5 33.1 all-gather.8
  324.1 54.3 reduce-scatter.8
  390.7 33.1 all-gather.10
  442.7 54.3 reduce-scatter.10
  499.5 54.2 reduce-scatter.6
  560.2 756.7 all-reduce.8
where the time goes:
time: 1360 us; the launch traced here: 1350 us
  waiting for transfers between devices  858 us (63%)
  blocking collectives  161 us (12%)
  matrix products  123 us (9%)
  local copies, waits for them, and re-layouts  113 us (8%)
  other arithmetic  44 us (3%)
  starting transfers between devices  38.6 us (3%)
  between operations  14.6 us (1%)
    psum x1, waiting for transfers between devices, on_device(): lax.psum((grad_gain_one, grad_in_weight, grad_conv_weight, grad_out_weigh...  474 us
    psum x1, blocking collectives, on_device(): lax.psum((grad_gain_one, grad_in_weight, grad_conv_weight, grad_out_weigh...  144 us
    all_to_all x1, waiting for transfers between devices, on_device(): lax.all_to_all(block_piece[local_ids], 'dp', split_axis=0, concat_axis=0,...  91.2 us
    reduce_scatter x1, waiting for transfers between devices, on_device(): lax.psum_scatter(normed_terms, 'mp', scatter_dimension=1, tiled=True)  54.4 us
    reduce_scatter x1, waiting for transfers between devices, on_device(): lax.psum_scatter(mix_terms, 'mp', scatter_dimension=1, tiled=True)  48.6 us
    reduce_scatter x1, waiting for transfers between devices, on_device(): lax.psum_scatter(down_terms, 'mp', scatter_dimension=1, tiled=True)  46.9 us
    all_gather x1, waiting for transfers between devices, on_device(): lax.all_gather(input_piece, 'mp', axis=1, tiled=True)  37.1 us
    unnamed x79, local copies, waits for them, and re-layouts  34.7 us
  transfers between devices with their start and end apart: 14, of which 11 were waited for; matrix products, arithmetic and copies ran while one was open for 11% of the time, Pallas kernels for 0%

commit v1 on v0

--- a/solution.py
+++ b/solution.py
@@ -45,6 +45,26 @@
     up_weight,
     down_weight,
 ):
+
+    def write_the_heaps(message):
+        outer = lax.psum(1, "dp")
+        low = lax.axis_index("dp")
+        local_now, shaped = (outer, low)
+        part_now = message.shape[0] // local_now
+        v_next = list(message.shape)
+        v_next[0] = part_now
+        aux = v_next[0]
+        v_next[0] = aux * local_now
+        y1 = jnp.zeros(v_next, message.dtype)
+        for u in [*range(local_now)]:
+            view_out = lax.dynamic_slice_in_dim(message, (shaped ^ u) * part_now, part_now, axis=0)
+            if u:
+                view_out = lax.ppermute(
+                    view_out, "dp", [(dev_i, dev_i ^ u) for dev_i in range(local_now)]
+                )
+            y1 = lax.dynamic_update_slice_in_dim(y1, view_out, (shaped ^ u) * aux, axis=0)
+        return y1
+
     dp_size = lax.axis_size("dp")
     mp_index = lax.axis_index("mp")
     row_count = tokens.shape[0]
@@ -201,7 +221,7 @@
     )
     local_ids = jnp.clip(got_places, 0, row_count - 1)
     back_out, back_grad = (
-        lax.all_to_all(block_piece[local_ids], "dp", split_axis=0, concat_axis=0, tiled=True),
+        write_the_heaps(block_piece[local_ids]),
         lax.all_to_all(input_grad[local_ids], "dp", split_axis=0, concat_axis=0, tiled=True),
     )
     home = jnp.where(filled, sources, row_count).reshape(-1)

time: 1360 us -> 1370 us (level)
  waiting for transfers between devices: 858 us -> 822 us
  blocking collectives: 161 us -> 180 us
  local copies, waits for them, and re-layouts: 113 us -> 129 us
    all_to_all x1 -> x0, waiting for transfers between devices: 91.2 us -> none  [on_device(): lax.all_to_all(block_piece[local_ids], 'dp', split_axis=0, concat_axis=0,...]
    ppermute x0 -> x15, waiting for transfers between devices: none -> 73.2 us  [write_the_heaps(): lax.ppermute(view_out, 'dp', [(dev_i, dev_i ^ u) for dev_i in range(local...]
    ppermute x0 -> x15, starting transfers between devices: none -> 19.7 us  [write_the_heaps(): lax.ppermute(view_out, 'dp', [(dev_i, dev_i ^ u) for dev_i in range(local...]
    psum x1, blocking collectives: 144 us -> 162 us  [on_device(): lax.psum((grad_gain_one, grad_in_weight, grad_conv_weight, grad_out_weigh...]
    psum x1, waiting for transfers between devices: 474 us -> 457 us  [on_device(): lax.psum((grad_gain_one, grad_in_weight, grad_conv_weight, grad_out_weigh...]
    unnamed x79 -> x93, local copies, waits for them, and re-layouts: 34.7 us -> 37.9 us
  transfers between devices with their start and end apart: 14 -> 28, of which waited for: 11 -> 19; matrix products, arithmetic and copies ran while one was open for 11% -> 11% of each run, Pallas kernels for 0% -> 0%
where the time goes in v1:
time: 1370 us; the launch traced here: 1360 us
  waiting for transfers between devices  822 us (60%)
  blocking collectives  180 us (13%)
  local copies, waits for them, and re-layouts  129 us (9%)
  matrix products  123 us (9%)
  starting transfers between devices  45.7 us (3%)
  other arithmetic  44 us (3%)
  between operations  14.7 us (1%)
    psum x1, waiting for transfers between devices, on_device(): lax.psum((grad_gain_one, grad_in_weight, grad_conv_weight, grad_out_weigh...  457 us
    psum x1, blocking collectives, on_device(): lax.psum((grad_gain_one, grad_in_weight, grad_conv_weight, grad_out_weigh...  162 us
    ppermute x15, waiting for transfers between devices, write_the_heaps(): lax.ppermute(view_out, 'dp', [(dev_i, dev_i ^ u) for dev_i in range(local...  73.2 us
    reduce_scatter x1, waiting for transfers between devices, on_device(): lax.psum_scatter(normed_terms, 'mp', scatter_dimension=1, tiled=True)  54.4 us
    reduce_scatter x1, waiting for transfers between devices, on_device(): lax.psum_scatter(mix_terms, 'mp', scatter_dimension=1, tiled=True)  48.6 us
    reduce_scatter x1, waiting for transfers between devices, on_device(): lax.psum_scatter(down_terms, 'mp', scatter_dimension=1, tiled=True)  46.3 us
    unnamed x93, local copies, waits for them, and re-layouts  37.9 us
    all_gather x1, waiting for transfers between devices, on_device(): lax.all_gather(input_piece, 'mp', axis=1, tiled=True)  37.1 us
  transfers between devices with their start and end apart: 28, of which 19 were waited for; matrix products, arithmetic and copies ran while one was open for 11% of the time, Pallas kernels for 0%

profile of v1, /device:TPU:0, one launch (start us, length us, event | category | flops | bytes accessed | tf_op | source)
XLA Modules:
  0.0 1359.0 jit_solution(17710249508894525925)
XLA Ops:
  63.2 30.1 %all-to-all-done.1 = bf16[16,96,512]{2,1,0:T(8,128)(2,1)} async-done(((bf16[16,96,512]{2,1,0:T(8,128)(2,1)}), bf16[16,96,512]{2,1,0:T(8,128)(2,1)}, u32[]{:S(2)}, u32[]{:S(2)}) %all-to-all-start.1) | async-done | bytes 1572896 | tf_op jit(solution)/shard_map/all_to_all | solution.py:91
  93.3 8.7 scatter_custom_fusion
  102.6 37.1 %all-gather.5.cloned.1.call-done = bf16[1024,1024]{1,0:T(8,128)(2,1)} async-done(((bf16[1024,512]{1,0:T(8,128)(2,1)}), bf16[1024,1024]{1,0:T(8,128)(2,1)}) %all-gather.5.cloned.1.call-update) | async-done | bytes 2097168 | tf_op jit(solution)/shard_map/all_gather | solution.py:107
  160.8 48.6 %reduce-scatter.5.cloned.1.call-done = f32[1024,512]{1,0:T(8,128)} async-done(((f32[1024,1024]{1,0:T(8,128)}), f32[1024,512]{1,0:T(8,128)}) %reduce-scatter.5.cloned.1.call-update) | async-done | bytes 2097168 | tf_op jit(solution)/shard_map/reduce_scatter | solution.py:126
  220.7 8.8 scatter_custom_fusion.2
  229.7 24.2 %all-gather.7.cloned.1.call-done = bf16[1024,1024]{1,0:T(8,128)(2,1)} async-done(((bf16[1024,512]{1,0:T(8,128)(2,1)}), bf16[1024,1024]{1,0:T(8,128)(2,1)}) %all-gather.7.cloned.1.call-update) | async-done | bytes 2097168 | tf_op jit(solution)/shard_map/all_gather | solution.py:130
  253.9 10.2 fusion.41
  264.1 9.9 fusion.40
  274.1 14.5 %all-gather.9.cloned.1.call-done = bf16[1024,1024]{1,0:T(8,128)(2,1)} async-done(((bf16[1024,512]{1,0:T(8,128)(2,1)}), bf16[1024,1024]{1,0:T(8,128)(2,1)}) %all-gather.9.cloned.1.call-update) | async-done | bytes 2097168 | tf_op jit(solution)/shard_map/all_gather | solution.py:108
  288.5 17.9 %multiply_convert_fusion = (bf16[1024,2304]{1,0:T(8,128)(2,1)}, bf16[1024,2304]{1,0:T(8,128)(2,1)}, bf16[1024,2304]{1,0:T(8,128)(2,1)}) fusion(f32[1024,2304]{1,0:T(8,128)} %fusion.40, f32[1024,2304]{1,0:T(8,128)} %fusion.41, bf16[1024,1024]{1,0:T(8,128)(2,1)} %all-gather.9.cloned.1.call-done, bf16[2304,1024]{1,0:T(8,128)(2,1)} %param.23), kind=kOutput, calls=%fused_computation.11 | convolution fusion | flops 4867227648 | bytes 39845888 | tf_op jit(solution)/shard_map/rd,fd->rf/dot_general | solution.py:140
  306.4 8.5 fusion.43
  314.9 9.0 convolution_add_fusion
  324.0 54.4 %reduce-scatter.9.cloned.1.call-done = f32[1024,512]{1,0:T(8,128)} async-done(((f32[1024,1024]{1,0:T(8,128)}), f32[1024,512]{1,0:T(8,128)}) %reduce-scatter.9.cloned.1.call-update) | async-done | bytes 2097168 | tf_op jit(solution)/shard_map/reduce_scatter | solution.py:154
  390.8 33.1 %all-gather.11.cloned.1.call-done = bf16[1024,1024]{1,0:T(8,128)(2,1)} async-done(((bf16[1024,512]{1,0:T(8,128)(2,1)}), bf16[1024,1024]{1,0:T(8,128)(2,1)}) %all-gather.11.cloned.1.call-update) | async-done | bytes 2097168 | tf_op jit(solution)/shard_map/all_gather | solution.py:169
  443.1 9.6 fusion.42
  453.0 10.3 fusion.47
  463.3 10.2 fusion.46
  473.5 10.3 fusion.45
  507.9 46.3 %reduce-scatter.7.cloned.1.call-done = f32[1024,512]{1,0:T(8,128)} async-done(((f32[1024,1024]{1,0:T(8,128)}), f32[1024,512]{1,0:T(8,128)}) %reduce-scatter.7.cloned.1.call-update) | async-done | bytes 2097168 | tf_op jit(solution)/shard_map/reduce_scatter | solution.py:137
  592.7 162.3 %all-reduce.4 = (f32[1024]{0:T(1024)}, f32[3,512]{1,0:T(4,128)}, f32[1024]{0:T(1024)}) all-reduce(f32[1024]{0:T(1024)} %get-tuple-element.68, f32[3,512]{1,0:T(4,128)S(1)} %pad_maximum_fusion.3, f32[1024]{0:T(1024)} %get-tuple-element.69), channel_id=1, replica_groups=mesh['dp'=16,'mp'=2] {'dp'}, use_global_device_ids=true, to_apply=%region_22.23 | all-reduce | flops 3584 | bytes 28672 | tf_op jit(solution)/shard_map/psum | solution.py:209
  804.4 14.8 %collective-permute-done.8 = f32[1,96,512]{2,1,0:T(8,128)S(1)} collective-permute-done((f32[1,96,512]{2,1,0:T(8,128)S(1)}, f32[1,96,512]{2,1,0:T(8,128)S(1)}, u32[]{:S(2)}, u32[]{:S(2)}) %collective-permute-start.8) | collective-permute-done | bytes 196640 | tf_op jit(solution)/shard_map/ppermute | solution.py:62
  819.9 14.1 %collective-permute-done.9 = f32[1,96,512]{2,1,0:T(8,128)S(1)} collective-permute-done((f32[1,96,512]{2,1,0:T(8,128)S(1)}, f32[1,96,512]{2,1,0:T(8,128)S(1)}, u32[]{:S(2)}, u32[]{:S(2)}) %collective-permute-start.9) | collective-permute-done | bytes 196640 | tf_op jit(solution)/shard_map/ppermute | solution.py:62
  857.8 9.0 scatter_custom_fusion.3
  866.8 456.6 %all-reduce.9.cloned.1.call-done = (f32[3,1024,512]{1,2,0:T(8,128)}, f32[512,1024]{1,0:T(8,128)}, f32[1024,2304]{1,0:T(8,128)}, f32[1024,2304]{1,0:T(8,128)}, f32[2304,1024]{1,0:T(8,128)}) async-done(((f32[3,1024,512]{1,2,0:T(8,128)}, f32[512,1024]{1,0:T(8,128)}, f32[1024,2304]{1,0:T(8,128)}, f32[1024,2304]{1,0:T(8,128)}, f32[2304,1024]{1,0:T(8,128)}), (f32[3,1024,512]{1,2,0:T(8,128)}, ...) | async-done | bytes 36700176 | tf_op jit(solution)/shard_map/psum | solution.py:209
  (245 shorter events, 285.8 us)
Async XLA Ops:
  30.7 24.4 %all-to-all-start = ((s32[16,1,96]{2,1,0:T(1,128)}), s32[16,1,96]{2,1,0:T(1,128)S(1)}, u32[]{:S(2)}, u32[]{:S(2)}) async-start(s32[16,1,96]{2,1,0:T(1,128)} %compare_select_fusion.4), calls=%async_computation | async-start | bytes 16384 | tf_op jit(solution)/shard_map/all_to_all | solution.py:93
  55.1 38.2 %all-to-all-start.1 = ((bf16[16,96,512]{2,1,0:T(8,128)(2,1)}), bf16[16,96,512]{2,1,0:T(8,128)(2,1)}, u32[]{:S(2)}, u32[]{:S(2)}) async-start(bf16[16,96,512]{2,1,0:T(8,128)(2,1)} %get-tuple-element.107), calls=%async_computation.1 | async-start | bytes 3145728 | tf_op jit(solution)/shard_map/all_to_all | solution.py:91
  61.3 78.5 %all-gather.5.cloned.1.call-start = ((), (), s32[]{:S(2)}) async-start(), calls=%async_computation.8 | async-start | bytes 3145728 | tf_op jit(solution)/shard_map/all_gather | solution.py:107
  102.1 107.3 %reduce-scatter.5.cloned.1.call-start = ((), (), s32[]{:S(2)}) async-start(), calls=%async_computation.9 | async-start | bytes 6291456 | tf_op jit(solution)/shard_map/reduce_scatter | solution.py:126
  155.0 65.7 %all-to-all-start.2 = ((bf16[16,96,512]{2,1,0:T(8,128)(2,1)}), bf16[16,96,512]{2,1,0:T(8,128)(2,1)}, u32[]{:S(2)}, u32[]{:S(2)}) async-start(bf16[16,96,512]{2,1,0:T(8,128)(2,1)} %get-tuple-element.106), calls=%async_computation.4 | async-start | bytes 3145728 | tf_op jit(solution)/shard_map/all_to_all | solution.py:92
  160.7 93.2 %all-gather.7.cloned.1.call-start = ((), (), s32[]{:S(2)}) async-start(), calls=%async_computation.10 | async-start | bytes 3145728 | tf_op jit(solution)/shard_map/all_gather | solution.py:130
  220.6 67.9 %all-gather.9.cloned.1.call-start = ((), (), s32[]{:S(2)}) async-start(), calls=%async_computation.12 | async-start | bytes 3145728 | tf_op jit(solution)/shard_map/all_gather | solution.py:108
  229.5 148.9 %reduce-scatter.9.cloned.1.call-start = ((), (), s32[]{:S(2)}) async-start(), calls=%async_computation.13 | async-start | bytes 6291456 | tf_op jit(solution)/shard_map/reduce_scatter | solution.py:154
  323.9 99.9 %all-gather.11.cloned.1.call-start = ((), (), s32[]{:S(2)}) async-start(), calls=%async_computation.14 | async-start | bytes 3145728 | tf_op jit(solution)/shard_map/all_gather | solution.py:169
  390.6 106.9 %reduce-scatter.11.cloned.1.call-start = ((), (), s32[]{:S(2)}) async-start(), calls=%async_computation.15 | async-start | bytes 6291456 | tf_op jit(solution)/shard_map/reduce_scatter | solution.py:195
  443.0 111.2 %reduce-scatter.7.cloned.1.call-start = ((), (), s32[]{:S(2)}) async-start(), calls=%async_computation.11 | async-start | bytes 6291456 | tf_op jit(solution)/shard_map/reduce_scatter | solution.py:137
  452.7 870.7 %all-reduce.9.cloned.1.call-start = ((), (), s32[]{:S(2)}) async-start(), calls=%async_computation.16 | async-start | bytes 73400320 | tf_op jit(solution)/shard_map/psum | solution.py:209
  566.9 291.0 %all-to-all-start.3 = ((f32[16,96,512]{2,1,0:T(8,128)}), f32[16,96,512]{2,1,0:T(8,128)}, u32[]{:S(2)}, u32[]{:S(2)}) async-start(f32[16,96,512]{2,1,0:T(8,128)} %bitcast.103), calls=%async_computation.7 | async-start | bytes 6291456 | tf_op jit(solution)/shard_map/all_to_all | solution.py:225
  583.0 171.9 %collective-permute-start = (f32[1,96,512]{2,1,0:T(8,128)}, f32[1,96,512]{2,1,0:T(8,128)S(1)}, u32[]{:S(2)}, u32[]{:S(2)}) collective-permute-start(f32[1,96,512]{2,1,0:T(8,128)} %get-tuple-element.94), channel_id=1, source_target_pairs={{0,2},{2,0},{4,6},{6,4},{8,10},{10,8},{12,14},{14,12},{16,18},{18,... | collective-permute-start | bytes 589832 | tf_op jit(solution)/shard_map/ppermute | solution.py:62
  583.4 172.3 %collective-permute-start.1 = (f32[1,96,512]{2,1,0:T(8,128)}, f32[1,96,512]{2,1,0:T(8,128)S(1)}, u32[]{:S(2)}, u32[]{:S(2)}) collective-permute-start(f32[1,96,512]{2,1,0:T(8,128)} %get-tuple-element.93), channel_id=1, source_target_pairs={{0,4},{2,6},{4,0},{6,2},{8,12},{10,14},{12,8},{14,10},{16,20},{18,... | collective-permute-start | bytes 589832 | tf_op jit(solution)/shard_map/ppermute | solution.py:62
  585.2 262.8 %collective-permute-start.14 = (f32[1,96,512]{2,1,0:T(8,128)S(1)}, f32[1,96,512]{2,1,0:T(8,128)S(1)}, u32[]{:S(2)}, u32[]{:S(2)}) collective-permute-start(f32[1,96,512]{2,1,0:T(8,128)S(1)} %get-tuple-element.80), channel_id=1, source_target_pairs={{0,30},{2,28},{4,26},{6,24},{8,22},{10,20},{12,18},{14,16},{16,14}... | collective-permute-start | bytes 589832 | tf_op jit(solution)/shard_map/ppermute | solution.py:62
  588.2 259.1 %collective-permute-start.13 = (f32[1,96,512]{2,1,0:T(8,128)S(1)}, f32[1,96,512]{2,1,0:T(8,128)S(1)}, u32[]{:S(2)}, u32[]{:S(2)}) collective-permute-start(f32[1,96,512]{2,1,0:T(8,128)S(1)} %get-tuple-element.81), channel_id=1, source_target_pairs={{0,28},{2,30},{4,24},{6,26},{8,20},{10,22},{12,16},{14,18},{16,12}... | collective-permute-start | bytes 589832 | tf_op jit(solution)/shard_map/ppermute | solution.py:62
  589.6 256.9 %collective-permute-start.12 = (f32[1,96,512]{2,1,0:T(8,128)}, f32[1,96,512]{2,1,0:T(8,128)S(1)}, u32[]{:S(2)}, u32[]{:S(2)}) collective-permute-start(f32[1,96,512]{2,1,0:T(8,128)} %get-tuple-element.82), channel_id=1, source_target_pairs={{0,26},{2,24},{4,30},{6,28},{8,18},{10,16},{12,22},{14,20},{16,10}... | collective-permute-start | bytes 589832 | tf_op jit(solution)/shard_map/ppermute | solution.py:62
  760.8 17.1 %collective-permute-start.4 = (f32[1,96,512]{2,1,0:T(8,128)}, f32[1,96,512]{2,1,0:T(8,128)S(1)}, u32[]{:S(2)}, u32[]{:S(2)}) collective-permute-start(f32[1,96,512]{2,1,0:T(8,128)} %get-tuple-element.90), channel_id=1, source_target_pairs={{0,10},{2,8},{4,14},{6,12},{8,2},{10,0},{12,6},{14,4},{16,26},{18,... | collective-permute-start | bytes 589832 | tf_op jit(solution)/shard_map/ppermute | solution.py:62
  769.8 16.5 %collective-permute-start.5 = (f32[1,96,512]{2,1,0:T(8,128)}, f32[1,96,512]{2,1,0:T(8,128)S(1)}, u32[]{:S(2)}, u32[]{:S(2)}) collective-permute-start(f32[1,96,512]{2,1,0:T(8,128)} %get-tuple-element.89), channel_id=1, source_target_pairs={{0,12},{2,14},{4,8},{6,10},{8,4},{10,6},{12,0},{14,2},{16,28},{18,... | collective-permute-start | bytes 589832 | tf_op jit(solution)/shard_map/ppermute | solution.py:62
  777.8 18.4 %collective-permute-start.6 = (f32[1,96,512]{2,1,0:T(8,128)}, f32[1,96,512]{2,1,0:T(8,128)S(1)}, u32[]{:S(2)}, u32[]{:S(2)}) collective-permute-start(f32[1,96,512]{2,1,0:T(8,128)} %get-tuple-element.88), channel_id=1, source_target_pairs={{0,14},{2,12},{4,10},{6,8},{8,6},{10,4},{12,2},{14,0},{16,30},{18,... | collective-permute-start | bytes 589832 | tf_op jit(solution)/shard_map/ppermute | solution.py:62
  796.3 23.0 %collective-permute-start.8 = (f32[1,96,512]{2,1,0:T(8,128)S(1)}, f32[1,96,512]{2,1,0:T(8,128)S(1)}, u32[]{:S(2)}, u32[]{:S(2)}) collective-permute-start(f32[1,96,512]{2,1,0:T(8,128)S(1)} %copy-done.24), channel_id=1, source_target_pairs={{0,18},{2,16},{4,22},{6,20},{8,26},{10,24},{12,30},{14,28},{16,2},... | collective-permute-start | bytes 589832 | tf_op jit(solution)/shard_map/ppermute | solution.py:62
  802.3 31.7 %collective-permute-start.9 = (f32[1,96,512]{2,1,0:T(8,128)S(1)}, f32[1,96,512]{2,1,0:T(8,128)S(1)}, u32[]{:S(2)}, u32[]{:S(2)}) collective-permute-start(f32[1,96,512]{2,1,0:T(8,128)S(1)} %copy-done.23), channel_id=1, source_target_pairs={{0,20},{2,22},{4,16},{6,18},{8,28},{10,30},{12,24},{14,26},{16,4},... | collective-permute-start | bytes 589832 | tf_op jit(solution)/shard_map/ppermute | solution.py:62
  819.2 25.9 %collective-permute-start.10 = (f32[1,96,512]{2,1,0:T(8,128)S(1)}, f32[1,96,512]{2,1,0:T(8,128)S(1)}, u32[]{:S(2)}, u32[]{:S(2)}) collective-permute-start(f32[1,96,512]{2,1,0:T(8,128)S(1)} %copy-done.22), channel_id=1, source_target_pairs={{0,22},{2,20},{4,18},{6,16},{8,30},{10,28},{12,26},{14,24},{16,6},... | collective-permute-start | bytes 589832 | tf_op jit(solution)/shard_map/ppermute | solution.py:62
  (48 other events, 1469.7 us)
Sparse Core Ops, SparseCore 0:
  102.2 37.5 all-gather.4
  155.1 54.2 reduce-scatter.4
  220.8 33.1 all-gather.6
  255.4 33.1 all-gather.8
  324.0 54.3 reduce-scatter.8
  390.7 33.1 all-gather.10
  443.2 54.2 reduce-scatter.10
  499.9 54.3 reduce-scatter.6
  560.7 762.6 all-reduce.8
